TPU v7x, 512 devices: a whole 4x4x16 slice. The times are simulated.
512 devices in a mesh: pool: 32 (over y, z_lo, core), col: 16 (over x, z_hi).
Axes of the slice: x: 4, y: 4, z: 16 (z_hi: 4, z_lo: 4; z = z_hi * 4 + z_lo), core: 2. Of those that a mesh axis runs over, the one named last changes fastest.
Arguments:
- matrix_elems: bfloat16 [512, 64, 32768], P(None, 'pool', 'col'), may hold values from -6 to 6
- residue: bfloat16 [1024, 32768], P('pool', 'col'), may hold values from -6 to 6
- pole_freq: bfloat16 [1024, 32768], P('pool', 'col'), may hold values from 0.5 to 4
- slab_index: int32 [1024], P('col'), may hold values from 0 to 32767, as said below
- band_order: int32 [64], replicated, may hold values from 0 to 63, each once
- band_mag: float32 [64], replicated, may hold values from 0.1 to 8
Outputs:
- self_energy: float32 [512, 512], P('col')
Inputs may be any that keep to these rules, and one draw needn't show every extreme that they name: Block i of slab_index (positions i * 64 to (i + 1) * 64 - 1) holds distinct increasing G-vectors of i * 2048 to (i + 1) * 2048 - 1.
All inputs are finite; a program needn't handle non-finite values.
Results may differ from a plain program's by a relative error of at most 0.004.
Values may be sent and summed in bfloat16 or wider, within the bound.
A program may use at most 128 MiB of HBM per device.

v0:
```python
import jax
import jax.numpy as jnp
from jax import lax
from jax.sharding import PartitionSpec as P

broadening = 0.25


def pole_weights(res_rows, pole_rows, magnitude, parity):
    detuning = pole_rows.astype(jnp.float32)[None] + magnitude[:, None, None]
    signed_gap = parity[:, None, None] * detuning
    scaled = (
        res_rows.astype(jnp.float32)[None]
        * signed_gap
        / (signed_gap * signed_gap + broadening * broadening)
    )
    return scaled.astype(jnp.bfloat16)


def on_device(matrix_elems, residue, pole_freq, slab_index, band_order, band_mag):
    pool_count = lax.axis_size("pool")
    col_count = lax.axis_size("col")
    pool_at = lax.axis_index("pool")
    col_at = lax.axis_index("col")
    band_total = band_order.shape[0]
    occupied = band_total // 4
    states = matrix_elems.shape[0]
    members = matrix_elems.shape[1]
    column_count = matrix_elems.shape[2]
    slab_total = residue.shape[0] * pool_count
    ordinals = lax.dynamic_slice_in_dim(band_order, pool_at * members, members)
    matches = ordinals[:, None] == jnp.arange(band_total, dtype=jnp.int32)[None, :]
    magnitude = jnp.sum(jnp.where(matches, band_mag[None, :], 0.0), axis=1)
    parity = jnp.where(ordinals < occupied, 1.0, -1.0).astype(jnp.float32)
    local_rows = slab_index - col_at * column_count
    picked = jnp.take(matrix_elems, local_rows, axis=2)
    slab_elems = lax.all_gather(picked, "col", axis=2, tiled=True)
    gathered_poles = lax.all_gather(pole_freq, "pool", axis=0, tiled=True)
    weights = pole_weights(
        lax.all_gather(residue, "pool", axis=0, tiled=True), gathered_poles, magnitude, parity
    )
    mixed_rows = jnp.einsum(
        "njr,jrg->jng", slab_elems, weights, preferred_element_type=jnp.float32
    ).astype(jnp.bfloat16)
    normalizer = 1.0 / jnp.sqrt(jnp.float32(band_total) * slab_total * column_count * col_count)
    running = jnp.zeros((states // col_count * lax.axis_size("col"), states), jnp.float32)
    for member in range(members):
        left_part = mixed_rows[member]
        running = running + lax.dot_general(
            left_part,
            matrix_elems[:, member, :],
            (((1,), (1,)), ((), ())),
            preferred_element_type=jnp.float32,
        )
    owned_rows = lax.psum_scatter(running * normalizer, "col", scatter_dimension=0, tiled=True)
    self_energy = lax.psum(owned_rows, "pool")
    return self_energy


def solution(mesh):
    placed = (P(None, "pool", "col"), P("pool", "col"), P("pool", "col"), P("col"), P(), P())
    return jax.shard_map(
        on_device, mesh=mesh, in_specs=placed, out_specs=P("col", None), check_vma=False
    )
```

profile of v0, /device:TPU:1, one launch (start us, length us, event | category | flops | bytes accessed | tf_op | source)
XLA Modules:
  0.0 632.1 jit_solution(1917082151361824840)
XLA Ops:
  6.5 0.0 all-gather.8.cloned.1.call-start
  6.5 0.7 all-gather.8.cloned.1.call-update
  7.3 0.0 all-gather.6.cloned.1.call-start
  7.3 0.7 all-gather.6.cloned.1.call-update
  8.0 0.0 all-gather.4.cloned.1.call-start
  8.1 0.0 copy-start.2
  8.1 0.0 copy-start.3
  8.1 0.0 copy-start.4
  8.1 16.0 %copy.11 = bf16[512,2,2048]{0,1,2:T(2,128)(2,1)} copy(bf16[512,2,2048]{2,1,0:T(2,128)(2,1)} %param.6) | data formatting | bytes 8388608 | tf_op args[0]
  24.1 0.0 copy-done.2
  24.1 3.0 gather_fusion
  27.2 0.7 fusion.11
  27.9 0.0 all-gather.4.cloned.1.call-update
  27.9 0.0 reduce-scatter.2.cloned.1.call-start
  28.0 0.0 copy-done.3
  28.0 0.1 compare_select_fusion.2
  28.1 0.0 copy-done.4
  28.1 0.2 fusion.12
  28.3 10.4 %fusion.14 = (bf16[512,1,2048]{2,1,0:T(2,128)(2,1)}, bf16[512,1,2048]{2,1,0:T(2,128)(2,1)}) fusion(bf16[512,2,2048]{2,1,0:T(2,128)(2,1)} %param.6), kind=kLoop, calls=%fused_computation.26 | loop fusion | bytes 8388608 | tf_op jit(solution)/shard_map/slice | solution.py:51
  38.6 44.7 %all-gather.8.cloned.1.call-done = bf16[1024,2048]{1,0:T(8,128)(2,1)} async-done(((bf16[32,2048]{1,0:T(8,128)(2,1)}), bf16[1024,2048]{1,0:T(8,128)(2,1)}) %all-gather.8.cloned.1.call-update) | async-done | bytes 4194320 | tf_op jit(solution)/shard_map/all_gather | solution.py:38
  83.3 6.5 %convert_element_type.13 = f32[1024,2048]{1,0:T(8,128)} convert(bf16[1024,2048]{1,0:T(8,128)(2,1)} %all-gather.8.cloned.1.call-done) | non-fusion elementwise | flops 2097152 | bytes 12582912 | tf_op jit(solution)/shard_map/convert_element_type | solution.py:10
  89.8 62.7 %all-gather.6.cloned.1.call-done = bf16[1024,2048]{1,0:T(8,128)(2,1)} async-done(((bf16[32,2048]{1,0:T(8,128)(2,1)}), bf16[1024,2048]{1,0:T(8,128)(2,1)}) %all-gather.6.cloned.1.call-update) | async-done | bytes 4194320 | tf_op jit(solution)/shard_map/all_gather | solution.py:40
  152.5 6.5 %convert_element_type.12 = f32[1024,2048]{1,0:T(8,128)} convert(bf16[1024,2048]{1,0:T(8,128)(2,1)} %all-gather.6.cloned.1.call-done) | non-fusion elementwise | flops 2097152 | bytes 12582912 | tf_op jit(solution)/shard_map/convert_element_type | solution.py:13
  159.0 89.5 %all-gather.4.cloned.1.call-done = bf16[512,2,1024]{0,2,1:T(8,128)(2,1)} async-done(((bf16[512,2,64]{0,2,1:T(8,128)(2,1)}), bf16[512,2,1024]{0,2,1:T(8,128)(2,1)}) %all-gather.4.cloned.1.call-update) | async-done | bytes 2097168 | tf_op jit(solution)/shard_map/all_gather | solution.py:37
  248.5 0.0 copy-start.1
  248.5 11.3 %fusion.6 = bf16[2,512,2048]{2,1,0:T(8,128)(2,1)S(1)} fusion(bf16[512,2,1024]{0,2,1:T(8,128)(2,1)} %all-gather.4.cloned.1.call-done, f32[2]{0:T(128)S(1)} %fusion.12, f32[1024,2048]{1,0:T(8,128)} %convert_element_type.13, f32[2]{0:T(128)S(1)} %get-tuple-element.5, f32[1024,2048]{1,0:T(8,128)} %convert_element_type.12), kind=kOutput, calls=%fused_computation.8 | convolution fusion | flops 4326424576 | bytes 23068688 | tf_op jit(solution)/shard_map/njr,jrg->jng/dot_general | solution.py:42
  259.8 0.0 copy-done.1
  259.9 0.0 copy-start
  259.9 1.7 fusion.7
  261.6 0.5 copy-done
  262.0 2.6 fusion.10
  264.7 0.0 reduce-scatter.2.cloned.1.call-update
  264.7 0.0 all-reduce.2.cloned.1.call-start
  264.7 108.6 %reduce-scatter.2.cloned.1.call-done = f32[32,512]{1,0:T(8,128)} async-done(((f32[512,512]{1,0:T(8,128)}), f32[32,512]{1,0:T(8,128)}) %reduce-scatter.2.cloned.1.call-update) | async-done | bytes 65552 | tf_op jit(solution)/shard_map/reduce_scatter | solution.py:55
  373.3 0.0 all-reduce.2.cloned.1.call-update
  373.3 250.8 %all-reduce.2.cloned.1.call-done = f32[32,512]{1,0:T(8,128)} async-done(((f32[32,512]{1,0:T(8,128)}), f32[32,512]{1,0:T(8,128)}) %all-reduce.2.cloned.1.call-update) | async-done | bytes 65552 | tf_op jit(solution)/shard_map/psum | solution.py:56
  624.1 1.5 copy.29
  (2 shorter events, 0.0 us)
Async XLA Ops:
  6.5 76.8 %all-gather.8.cloned.1.call-start = ((), (), s32[]{:S(2)}) async-start(), calls=%async_computation.3 | async-start | bytes 4325376 | tf_op jit(solution)/shard_map/all_gather | solution.py:38
  7.3 145.2 %all-gather.6.cloned.1.call-start = ((), (), s32[]{:S(2)}) async-start(), calls=%async_computation.2 | async-start | bytes 4325376 | tf_op jit(solution)/shard_map/all_gather | solution.py:40
  8.0 240.5 %all-gather.4.cloned.1.call-start = ((), (), s32[]{:S(2)}) async-start(), calls=%async_computation.1 | async-start | bytes 2228224 | tf_op jit(solution)/shard_map/all_gather | solution.py:37
  8.1 16.1 %copy-start.2 = (s32[64]{0:T(128)S(1)}, s32[64]{0:T(128)}, u32[]{:S(2)}) copy-start(s32[64]{0:T(128)} %param.9) | copy-start | bytes 772
  8.1 19.9 %copy-start.3 = (s32[64]{0:T(128)S(1)}, s32[64]{0:T(128)}, u32[]{:S(2)}) copy-start(s32[64]{0:T(128)} %param.10) | copy-start | bytes 772
  8.1 20.0 %copy-start.4 = (f32[64]{0:T(128)S(1)}, f32[64]{0:T(128)}, u32[]{:S(2)}) copy-start(f32[64]{0:T(128)} %param.11) | copy-start | bytes 772
  27.9 345.4 %reduce-scatter.2.cloned.1.call-start = ((), (), s32[]{:S(2)}) async-start(), calls=%async_computation.4 | async-start | bytes 1114112 | tf_op jit(solution)/shard_map/reduce_scatter | solution.py:55
  248.5 11.3 %copy-start.1 = (bf16[512,1,2048]{2,1,0:T(2,128)(2,1)S(1)}, bf16[512,1,2048]{2,1,0:T(2,128)(2,1)}, u32[]{:S(2)}) copy-start(bf16[512,1,2048]{2,1,0:T(2,128)(2,1)} %get-tuple-element.10) | copy-start | bytes 6291460
  259.9 2.2 copy-start
  264.7 359.4 %all-reduce.2.cloned.1.call-start = ((), (), s32[]{:S(2)}) async-start(), calls=%async_computation.5 | async-start | bytes 131072 | tf_op jit(solution)/shard_map/psum | solution.py:56
Sparse Core Ops, SparseCore 0:
  9.5 73.7 all-gather.7
  85.4 66.9 all-gather.5
  155.5 92.9 all-gather.3
  264.8 108.4 reduce-scatter.1
  376.3 247.7 all-reduce.1
where the time goes:
time: 634 us; the launch traced here: 632 us
  waiting for transfers between devices  558 us (88%)
  local copies, waits for them, and re-layouts  31.4 us (5%)
  matrix products  15.6 us (2%)
  other arithmetic  14 us (2%)
  between operations  13.2 us (2%)
    psum x1, waiting for transfers between devices, on_device(): self_energy = lax.psum(owned_rows, 'pool')  251 us
    reduce_scatter x1, waiting for transfers between devices, on_device(): lax.psum_scatter(running * normalizer, 'col', scatter_dimension=0, tiled=...  109 us
    all_gather x1, waiting for transfers between devices, on_device(): slab_elems = lax.all_gather(picked, 'col', axis=2, tiled=True)  89.5 us
    all_gather x1, waiting for transfers between devices, on_device(): lax.all_gather(residue, 'pool', axis=0, tiled=True)  62.7 us
    all_gather x1, waiting for transfers between devices, on_device(): gathered_poles = lax.all_gather(pole_freq, 'pool', axis=0, tiled=True)  44.7 us
    unnamed x12, local copies, waits for them, and re-layouts  18 us
  transfers between devices with their start and end apart: 5, of which 5 were waited for; matrix products, arithmetic and copies ran while one was open for 7% of the time, Pallas kernels for 0%

commit v1 on v0

v1 whole, which is shorter than its diff:
```python
import jax
import jax.numpy as jnp
from jax import lax
from jax.experimental import pallas as pl
from jax.experimental.pallas import tpu as pltpu
from jax.sharding import PartitionSpec as P

broadening = 0.25
SIDE = 4


class Place:
    def __init__(self):
        pool, col = lax.axis_index("pool"), lax.axis_index("col")
        self.y, self.z, self.c = pool // 8, (pool // 2) % 4, pool % 2
        self.x, self.h = col // 4, col % 4

    def at(self, **moved):
        y, z, c, x, h = (moved.get(k, getattr(self, k)) for k in "yzcxh")
        return ((y * 4 + z) * 2 + c, x * 4 + h)


def ring(at, by):
    return lax.rem(at + by + SIDE, SIDE)


class Sends:
    def __init__(self, sems):
        self.sems, self.count, self.kept = sems, 0, []

    def start(self, src, dst, recv_sem, device, when=None):
        slot = self.count
        self.count += 1

        def made():
            return pltpu.make_async_remote_copy(
                src_ref=src(), dst_ref=dst(), send_sem=self.sems.at[slot], recv_sem=recv_sem(),
                device_id=device, device_id_type=pl.DeviceIdType.MESH)

        if when is None:
            made().start()
        else:
            pl.when(when)(lambda: made().start())
        self.kept.append((made, when))

    def finish(self):
        for made, when in self.kept:
            if when is None:
                made().wait_send()
            else:
                pl.when(when)(lambda made=made: made().wait_send())


def arrived(view, sem, device):
    pltpu.make_async_remote_copy(
        src_ref=view, dst_ref=view, send_sem=sem, recv_sem=sem,
        device_id=device, device_id_type=pl.DeviceIdType.MESH).wait_recv()


def greet(devices):
    barrier = pltpu.get_barrier_semaphore()
    total = jnp.int32(0)
    for device, when in devices:
        def signal(device=device):
            pl.semaphore_signal(
                barrier, inc=1, device_id=device, device_id_type=pl.DeviceIdType.MESH)
        if when is None:
            signal()
            total = total + 1
        else:
            pl.when(when)(signal)
            total = total + when.astype(jnp.int32)
    pl.semaphore_wait(barrier, total)


def gather_partners(me):
    pairs = [(me.at(c=1 - me.c), None)]
    for by in (1, -1):
        pairs += [(me.at(y=ring(me.y, by)), None), (me.at(x=ring(me.x, by)), None),
                  (me.at(h=ring(me.h, by)), None)]
    pairs += [(me.at(z=me.z + 1), me.z < 3), (me.at(z=me.z - 1), me.z > 0)]
    return pairs


def gather_steps(me, sends, own, full, pick, slab, pole_sems, twin_sems, slab_sems):
    rows, depth = own[0].shape[0], pick.shape[1]

    def pole_view(half, y, z, c):
        at = ((y * 4 + z) * 2 + c) * rows
        return full[half].at[pl.ds(pl.multiple_of(at, rows), rows)]

    def pole_source(half, y, z, mine):
        return own[half] if mine else pole_view(half, y, z, me.c)

    def send_pole(half, y, z, device, when=None, mine=False):
        sends.start(lambda: pole_source(half, y, z, mine), lambda: pole_view(half, y, z, me.c),
                    lambda: pole_sems.at[(y * 4 + z) * 2 + half], device, when)

    def send_twin(half, y, z, when=None, mine=False):
        sends.start(lambda: pole_source(half, y, z, mine), lambda: pole_view(half, y, z, me.c),
                    lambda: twin_sems.at[(y * 4 + z) * 2 + half], me.at(c=1 - me.c), when)

    def await_pole(half, y, z, when=None):
        def waits():
            arrived(pole_view(half, y, z, me.c), pole_sems.at[(y * 4 + z) * 2 + half], me.at(c=1 - me.c))
        waits() if when is None else pl.when(when)(waits)

    def await_twin(half, y, z):
        arrived(pole_view(half, y, z, 1 - me.c), twin_sems.at[(y * 4 + z) * 2 + half], me.at(c=1 - me.c))

    def slab_view(half, x, h):
        return slab.at[half, pl.ds(pl.multiple_of((x * 4 + h) * depth, depth), depth)]

    def send_slab(half, x, h, device, mine=False):
        sends.start(lambda: pick.at[half] if mine else slab_view(half, x, h),
                    lambda: slab_view(half, x, h), lambda: slab_sems.at[(x * 4 + h) * 2 + half], device)

    def await_slab(half, x, h):
        arrived(slab_view(half, x, h), slab_sems.at[(x * 4 + h) * 2 + half], me.at(c=1 - me.c))

    up, down = me.at(y=ring(me.y, 1)), me.at(y=ring(me.y, -1))
    east, west = me.at(x=ring(me.x, 1)), me.at(x=ring(me.x, -1))
    far, near = me.at(h=ring(me.h, 1)), me.at(h=ring(me.h, -1))
    right, left = me.at(z=me.z + 1), me.at(z=me.z - 1)

    def along_y(z, when=None, mine=False):
        for half in (0, 1):
            send_pole(half, me.y, z, up, when, mine)
            send_pole(half, me.y, z, down, when, mine)

    def to_twin(y, z, when=None, mine=False):
        for half in (0, 1):
            send_twin(half, y, z, when, mine)

    def from_y(z, when=None):
        below, above = ring(me.y, -1), ring(me.y, 1)
        await_pole(0, below, z, when)
        send_pole(0, below, z, up, when)
        await_pole(1, above, z, when)
        send_pole(1, above, z, down, when)
        await_pole(1, below, z, when)
        await_pole(0, above, z, when)
        to_twin(below, z, when)
        to_twin(above, z, when)

    def from_opposite(z, when=None):
        across = ring(me.y, 2)
        for half in (0, 1):
            await_pole(half, across, z, when)
            send_twin(half, across, z, when)

    def from_z(by):
        for sign, onward, can in ((-1, right, me.z < 3), (1, left, me.z > 0)):
            z = me.z + sign * by
            there = (z >= 0) & (z <= 3)
            for half in (0, 1):
                await_pole(half, me.y, z, there)
                if by < 3:
                    send_pole(half, me.y, z, onward, there & can)
            along_y(z, there)
            to_twin(me.y, z, there)

    def sources(by):
        return [(z, (z >= 0) & (z <= 3)) for z in (me.z - by, me.z + by)]

    def along_x(h, mine=False):
        for half in (0, 1):
            send_slab(half, me.x, h, east, mine)
            send_slab(half, me.x, h, west, mine)

    def from_x(h):
        behind, ahead = ring(me.x, -1), ring(me.x, 1)
        await_slab(0, behind, h)
        send_slab(0, behind, h, east)
        await_slab(1, ahead, h)
        send_slab(1, ahead, h, west)
        await_slab(1, behind, h)
        await_slab(0, ahead, h)

    def from_x_opposite(h):
        for half in (0, 1):
            await_slab(half, ring(me.x, 2), h)

    behind, ahead, across = ring(me.h, -1), ring(me.h, 1), ring(me.h, 2)

    def first():
        for half in (0, 1):
            send_pole(half, me.y, me.z, right, me.z < 3, True)
            send_pole(half, me.y, me.z, left, me.z > 0, True)
        along_y(me.z, None, True)
        to_twin(me.y, me.z, None, True)

    def slab_first():
        for half in (0, 1):
            send_slab(half, me.x, me.h, far, True)
            send_slab(half, me.x, me.h, near, True)
        along_x(me.h, True)

    def slab_second():
        await_slab(0, me.x, behind)
        send_slab(0, me.x, behind, far)
        await_slab(1, me.x, ahead)
        send_slab(1, me.x, ahead, near)
        await_slab(1, me.x, behind)
        await_slab(0, me.x, ahead)
        along_x(behind)
        along_x(ahead)

    def slab_third():
        for half in (0, 1):
            await_slab(half, me.x, across)
        along_x(across)

    def rest():
        from_z(1)
        from_y(me.z)
        slab_second()
        from_x(me.h)
        from_z(2)
        from_opposite(me.z)
        for z, there in sources(1):
            from_y(z, there)
        from_z(3)
        slab_third()
        from_x(behind)
        from_x(ahead)
        from_x_opposite(me.h)
        for z, there in sources(1):
            from_opposite(z, there)
        for z, there in sources(2):
            from_y(z, there)
        from_x(across)
        for h in (behind, ahead, across):
            from_x_opposite(h)
        for z, there in sources(3):
            from_y(z, there)
        for by in (2, 3):
            for z, there in sources(by):
                from_opposite(z, there)
        for y in range(SIDE):
            for z in range(SIDE):
                for half in (0, 1):
                    await_twin(half, y, z)

    return first, slab_first, rest


GATHER_SENDS = 220


def gather_kernel(pole, res, pick, poles, ress, slab, send_sems, pole_sems, twin_sems, slab_sems, own_sem):
    me = Place()
    rows, depth = pole.shape[0], pick.shape[1]
    greet(gather_partners(me))
    sends = Sends(send_sems)
    first, slab_first, rest = gather_steps(
        me, sends, (pole, res), (poles, ress), pick, slab, pole_sems, twin_sems, slab_sems)
    first()
    slab_first()
    at = pl.multiple_of(((me.y * 4 + me.z) * 2 + me.c) * rows, rows)
    poles[pl.ds(at, rows)] = pole[...]
    ress[pl.ds(at, rows)] = res[...]
    for half in (0, 1):
        slab[half, pl.ds(pl.multiple_of((me.x * 4 + me.h) * depth, depth), depth)] = pick[half]
    rest()
    sends.finish()


def gathered(pole, res, pick):
    dma = pltpu.SemaphoreType.DMA
    vmem = pl.BlockSpec(memory_space=pltpu.VMEM)
    rows, width = pole.shape
    return pl.pallas_call(
        gather_kernel,
        out_shape=(
            jax.ShapeDtypeStruct((rows * 32, width), pole.dtype),
            jax.ShapeDtypeStruct((rows * 32, width), res.dtype),
            jax.ShapeDtypeStruct((2, pick.shape[1] * 16, pick.shape[2]), pick.dtype),
        ),
        in_specs=[vmem] * 3,
        out_specs=(vmem,) * 3,
        scratch_shapes=[dma((GATHER_SENDS,)), dma((32,)), dma((32,)), dma((32,)), dma((1,))],
        compiler_params=pltpu.CompilerParams(
            collective_id=0, has_side_effects=True, vmem_limit_bytes=48 * 2**20),
    )(pole, res, pick)


def reduce_partners(me):
    pairs = [(me.at(c=1 - me.c), None)]
    for by in (1, 2, 3):
        y = ring(me.y, by)
        pairs += [(me.at(x=ring(me.x, by)), None), (me.at(h=ring(me.h, by)), None),
                  (me.at(z=ring(me.z, by)), None), (me.at(y=y), None), (me.at(y=y, c=1 - me.c), None)]
    return pairs


REDUCE_SENDS = 20


def reduce_steps(me, sends, part, out, mine, twin, x_in, x_sum, y_in, y_sum, h_in, z_all, last, sems):
    other = me.at(c=1 - me.c)

    def await_(view, slot):
        arrived(view, sems.at[slot], other)

    def send(src, dst, slot, device):
        sends.start(lambda: src, lambda: dst, lambda: sems.at[slot], device)

    width = mine.shape[-1]
    theirs = pl.ds(pl.multiple_of((1 - me.c) * width, width), width)
    ours = pl.ds(pl.multiple_of(me.c * width, width), width)
    for by in (1, 2, 3, 0):
        x = ring(me.x, by)
        block = pl.ds(pl.multiple_of(x * 128, 128), 128)
        send(part.at[block, theirs], twin.at[x], by, other)
    for by in (1, 2, 3, 0):
        x = ring(me.x, by)
        block = pl.ds(pl.multiple_of(x * 128, 128), 128)
        await_(twin.at[x], by)
        summed = part[block, ours] + twin[x]
        if by:
            mine[x] = summed
            send(mine.at[x], x_in.at[by - 1], 4 + by - 1, me.at(x=x))
        else:
            x_sum[...] = summed.reshape(x_sum.shape)
    total = x_sum[...]
    for by in (3, 1, 2):
        await_(x_in.at[by - 1], 4 + by - 1)
        total = total + x_in[by - 1].reshape(x_sum.shape)
    x_sum[...] = total
    for by in (2, 1, 3):
        y = ring(me.y, by)
        send(x_sum.at[:, y], y_in.at[by - 1], 7 + by - 1, me.at(y=y))
    total = x_sum[:, me.y]
    for by in (3, 1, 2):
        await_(y_in.at[by - 1], 7 + by - 1)
        total = total + y_in[by - 1]
    y_sum[...] = total
    for by in (2, 1, 3):
        h = ring(me.h, by)
        send(y_sum.at[h], h_in.at[by - 1], 10 + by - 1, me.at(h=h))
    total = y_sum[me.h]
    for by in (3, 1, 2):
        await_(h_in.at[by - 1], 10 + by - 1)
        total = total + h_in[by - 1]
    z_all[me.z] = total
    for by in (2, 1, 3):
        z = ring(me.z, by)
        send(z_all.at[me.z], z_all.at[me.z], 13 + me.z, me.at(z=z))
    for by in (3, 1, 2):
        z = ring(me.z, by)
        await_(z_all.at[z], 13 + z)
    last[...] = (z_all[0] + z_all[1]) + (z_all[2] + z_all[3])
    rows = pl.ds(pl.multiple_of(me.y * 8, 8), 8)
    slot = 17 + me.y * 2 + me.c
    for by in (2, 1, 3):
        y = ring(me.y, by)
        send(last, out.at[rows, ours], slot, me.at(y=y))
        send(last, out.at[rows, ours], slot, me.at(y=y, c=1 - me.c))
    send(last, out.at[rows, ours], slot, other)
    out[rows, ours] = last[...]
    for by in (0, 1, 2, 3):
        y = ring(me.y, by)
        there = pl.ds(pl.multiple_of(y * 8, 8), 8)
        if by:
            await_(out.at[there, ours], 17 + y * 2 + me.c)
        await_(out.at[there, theirs], 17 + y * 2 + 1 - me.c)


def reduce_scratch():
    f32 = jnp.float32
    return [
        pltpu.VMEM((4, 128, 256), f32), pltpu.VMEM((4, 128, 256), f32),
        pltpu.VMEM((3, 128, 256), f32), pltpu.VMEM((4, 4, 8, 256), f32),
        pltpu.VMEM((3, 4, 8, 256), f32), pltpu.VMEM((4, 8, 256), f32),
        pltpu.VMEM((3, 8, 256), f32), pltpu.VMEM((4, 8, 256), f32),
        pltpu.VMEM((8, 256), f32), pltpu.SemaphoreType.DMA((25,)),
    ]


def reduce_kernel(part, out, send_sems, *scratch):
    me = Place()
    greet(reduce_partners(me))
    sends = Sends(send_sems)
    reduce_steps(me, sends, part, out, *scratch)
    sends.finish()


def reduced(part):
    vmem = pl.BlockSpec(memory_space=pltpu.VMEM)
    return pl.pallas_call(
        reduce_kernel,
        out_shape=jax.ShapeDtypeStruct((32, part.shape[1]), jnp.float32),
        in_specs=[vmem],
        out_specs=vmem,
        scratch_shapes=[pltpu.SemaphoreType.DMA((32,))] + reduce_scratch(),
        compiler_params=pltpu.CompilerParams(collective_id=1, has_side_effects=True),
    )(part)


def pole_weights(res_rows, pole_rows, magnitude, parity):
    detuning = pole_rows.astype(jnp.float32)[None] + magnitude[:, None, None]
    signed_gap = parity[:, None, None] * detuning
    scaled = (
        res_rows.astype(jnp.float32)[None]
        * signed_gap
        / (signed_gap * signed_gap + broadening * broadening)
    )
    return scaled.astype(jnp.bfloat16)


def on_device(matrix_elems, residue, pole_freq, slab_index, band_order, band_mag):
    pool_at = lax.axis_index("pool")
    col_at = lax.axis_index("col")
    band_total = band_order.shape[0]
    occupied = band_total // 4
    members = matrix_elems.shape[1]
    column_count = matrix_elems.shape[2]
    slab_total = residue.shape[0] * lax.axis_size("pool")
    ordinals = lax.dynamic_slice_in_dim(band_order, pool_at * members, members)
    matches = ordinals[:, None] == jnp.arange(band_total, dtype=jnp.int32)[None, :]
    magnitude = jnp.sum(jnp.where(matches, band_mag[None, :], 0.0), axis=1)
    parity = jnp.where(ordinals < occupied, 1.0, -1.0).astype(jnp.float32)
    local_rows = slab_index - col_at * column_count
    chosen = (local_rows[:, None] == jnp.arange(column_count, dtype=jnp.int32)[None, :]).astype(jnp.bfloat16)
    picked = jnp.einsum(
        "rg,njg->jrn", chosen, matrix_elems, preferred_element_type=jnp.float32
    ).astype(jnp.bfloat16)
    poles, residues, slab_elems = gathered(pole_freq, residue, picked)
    weights = pole_weights(residues, poles, magnitude, parity)
    mixed_rows = jnp.einsum(
        "jrn,jrg->jng", slab_elems, weights, preferred_element_type=jnp.float32
    ).astype(jnp.bfloat16)
    normalizer = 1.0 / jnp.sqrt(
        jnp.float32(band_total) * slab_total * column_count * lax.axis_size("col"))
    part = jnp.einsum(
        "jng,mjg->nm", mixed_rows, matrix_elems, preferred_element_type=jnp.float32)
    return reduced(part * normalizer)


def solution(mesh):
    placed = (P(None, "pool", "col"), P("pool", "col"), P("pool", "col"), P("col"), P(), P())
    return jax.shard_map(
        on_device, mesh=mesh, in_specs=placed, out_specs=P("col", None), check_vma=False
    )
```

time: 634 us -> 142 us (0.22)
  waiting for transfers between devices: 558 us -> 0 us
  Pallas kernels: 0 us -> 106 us
  local copies, waits for them, and re-layouts: 31.4 us -> 3.29 us
  between operations: 13.2 us -> 0.04 us
    psum x1 -> x0, waiting for transfers between devices: 251 us -> none  [on_device(): self_energy = lax.psum(owned_rows, 'pool')]
    all_gather x3 -> x0, waiting for transfers between devices: 197 us -> none  [the longest x1 89.5 us: on_device(): slab_elems = lax.all_gather(picked, 'col', axis=2, tiled=True)]
    reduce_scatter x1 -> x0, waiting for transfers between devices: 109 us -> none  [on_device(): lax.psum_scatter(running * normalizer, 'col', scatter_dimension=0, tiled=...]
    pallas_call x0 -> x2, Pallas kernels: none -> 106 us  [the longest x1 71.1 us: gathered(): pl.pallas_call(gather_kernel, out_shape=(jax.ShapeDtypeStruct((rows * 32,...]
    unnamed x12 -> x7, local copies, waits for them, and re-layouts: 18 us -> 3.29 us
    slice x1 -> x0, local copies, waits for them, and re-layouts: 10.4 us -> none  [on_device(): matrix_elems[:, member, :]]
    dot_general x3 -> x2, matrix products: 15.6 us -> 19.5 us  [the longest x1 14.8 us: on_device(): jnp.einsum('jng,mjg->nm', mixed_rows, matrix_elems, preferred_element_typ...]
  transfers between devices with their start and end apart: 5 -> 0, of which waited for: 5 -> 0; matrix products, arithmetic and copies ran while one was open for 7% -> 0% of each run, Pallas kernels for 0% -> 0%
where the time goes in v1:
time: 142 us
  Pallas kernels  106 us (75%)
  matrix products  19.5 us (14%)
  other arithmetic  13.1 us (9%)
  local copies, waits for them, and re-layouts  3.29 us (2%)
    pallas_call x1, Pallas kernels, gathered(): pl.pallas_call(gather_kernel, out_shape=(jax.ShapeDtypeStruct((rows * 32,...  71.1 us
    pallas_call x1, Pallas kernels, reduced(): pl.pallas_call(reduce_kernel, out_shape=jax.ShapeDtypeStruct((32, part.sh...  35.2 us
    dot_general x1, matrix products, on_device(): jnp.einsum('jng,mjg->nm', mixed_rows, matrix_elems, preferred_element_typ...  14.8 us
    convert_element_type x1, other arithmetic, pole_weights(): res_rows.astype(jnp.float32)[None] * signed_gap  6.64 us
    dot_general x1, matrix products, on_device(): jnp.einsum('rg,njg->jrn', chosen, matrix_elems, preferred_element_type=jn...  4.67 us
    convert_element_type x1, other arithmetic, pole_weights(): detuning = pole_rows.astype(jnp.float32)[None] + magnitude[:, None, None]  4.28 us
    unnamed x7, local copies, waits for them, and re-layouts  3.29 us

profile of v1, /device:TPU:1, one launch (start us, length us, event | category | flops | bytes accessed | tf_op | source)
XLA Modules:
  0.0 142.2 jit_solution(3065301560525084865)
XLA Ops:
  0.0 0.7 broadcast_subtract_fusion
  0.7 0.7 compare_select_fusion.1
  1.4 0.8 fusion.30
  2.2 4.7 %fusion.24.pick = bf16[2,64,512]{2,1,0:T(8,128)(2,1)S(1)} fusion(bf16[512,2,2048]{2,1,0:T(2,128)(2,1)} %param.6, s32[64]{0:T(128)S(1)} %broadcast_subtract_fusion), kind=kOutput, calls=%fused_computation.15 | convolution fusion | flops 268632064 | bytes 4325632 | tf_op jit(solution)/shard_map/rg,njg->jrn/dot_general | solution.py:426
  6.9 0.0 copy-start
  6.9 0.9 copy-done
  7.8 0.0 copy-start.1
  7.8 0.9 copy-done.1
  8.7 71.1 %shard_map.64 = (bf16[1024,2048]{1,0:T(8,128)(2,1)}, bf16[1024,2048]{1,0:T(8,128)(2,1)}, bf16[2,1024,512]{2,1,0:T(8,128)(2,1)S(1)}) custom-call(bf16[32,2048]{1,0:T(8,128)(2,1)S(1)} %copy-done, bf16[32,2048]{1,0:T(8,128)(2,1)S(1)} %copy-done.1, bf16[2,64,512]{2,1,0:T(8,128)(2,1)S(1)} %fusion.24.pick), custom_call_target="tpu_custom_call" | custom-call | tf_op jit(solution)/shard_map/pallas_call | solution.py:273
  79.8 0.0 copy-start.2
  79.8 6.6 %convert_element_type.20 = f32[1024,2048]{1,0:T(8,128)} convert(bf16[1024,2048]{1,0:T(8,128)(2,1)} %get-tuple-element.9) | non-fusion elementwise | flops 2097152 | bytes 12582912 | tf_op jit(solution)/shard_map/convert_element_type | solution.py:405
  86.4 0.0 copy-done.2
  86.4 4.3 %convert_element_type.21 = f32[1024,2048]{1,0:T(8,128)} convert(bf16[1024,2048]{1,0:T(8,128)(2,1)S(1)} %copy-done.2) | non-fusion elementwise | flops 2097152 | bytes 12582912 | tf_op jit(solution)/shard_map/convert_element_type | solution.py:402
  90.7 14.8 %fusion.16.part = f32[512,512]{1,0:T(8,128)} fusion(bf16[512,2,2048]{2,1,0:T(2,128)(2,1)} %param.6, bf16[2,1024,512]{2,1,0:T(8,128)(2,1)S(1)} %get-tuple-element.8, f32[2]{0:T(128)S(1)} %fusion.30, f32[1024,2048]{1,0:T(8,128)} %convert_element_type.21, f32[2]{0:T(128)S(1)} %get-tuple-element.11, f32[1024,2048]{1,0:T(8,128)} %convert_element_type.20), kind=kOutput, calls=%fused_computation.13 | convolution fusion | flops 6474170368 | bytes 24117264 | tf_op jit(solution)/shard_map/jng,mjg->nm/dot_general | solution.py:436
  105.5 35.2 %shard_map.65 = f32[32,512]{1,0:T(8,128)} custom-call(f32[512,512]{1,0:T(8,128)} %fusion.16.part), custom_call_target="tpu_custom_call" | custom-call | tf_op jit(solution)/shard_map/pallas_call | solution.py:391
  140.7 1.5 %copy.24 = f32[32,512]{1,0:T(8,128)} copy(f32[32,512]{1,0:T(8,128)} %shard_map.65) | data formatting | bytes 131072
Async XLA Ops:
  6.9 0.9 copy-start
  7.8 0.9 copy-start.1
  79.8 6.6 %copy-start.2 = (bf16[1024,2048]{1,0:T(8,128)(2,1)S(1)}, bf16[1024,2048]{1,0:T(8,128)(2,1)}, u32[]{:S(2)}) copy-start(bf16[1024,2048]{1,0:T(8,128)(2,1)} %get-tuple-element.10) | copy-start | bytes 12582916

commit v2 on v1

v2 whole, which is shorter than its diff:
```python
import functools

import jax
import jax.numpy as jnp
import numpy as np
from jax import lax
from jax.experimental import pallas as pl
from jax.experimental.pallas import tpu as pltpu
from jax.sharding import PartitionSpec as P

broadening = 0.25
SIDE = 4
SENDS = 200


class Place:
    def __init__(self):
        pool, col = lax.axis_index("pool"), lax.axis_index("col")
        self.y, self.z, self.c = pool // 8, (pool // 2) % 4, pool % 2
        self.x, self.h = col // 4, col % 4

    def at(self, **moved):
        y, z, c, x, h = (moved.get(k, getattr(self, k)) for k in "yzcxh")
        return ((y * 4 + z) * 2 + c, x * 4 + h)


def ring(at, by):
    return lax.rem(at + by + SIDE, SIDE)


class Sends:
    def __init__(self, sems):
        self.sems, self.count, self.kept = sems, 0, []

    def start(self, src, dst, recv_sem, device, when=None):
        slot = self.count
        self.count += 1

        def made():
            return pltpu.make_async_remote_copy(
                src_ref=src(), dst_ref=dst(), send_sem=self.sems.at[slot], recv_sem=recv_sem(),
                device_id=device, device_id_type=pl.DeviceIdType.MESH)

        if when is None:
            made().start()
        else:
            pl.when(when)(lambda: made().start())
        self.kept.append((made, when))

    def finish(self):
        for made, when in self.kept:
            if when is None:
                made().wait_send()
            else:
                pl.when(when)(lambda made=made: made().wait_send())


def arrived(view, sem, device):
    pltpu.make_async_remote_copy(
        src_ref=view, dst_ref=view, send_sem=sem, recv_sem=sem,
        device_id=device, device_id_type=pl.DeviceIdType.MESH).wait_recv()


def greet(devices):
    barrier = pltpu.get_barrier_semaphore()
    total = jnp.int32(0)
    for device, when in devices:
        def signal(device=device):
            pl.semaphore_signal(
                barrier, inc=1, device_id=device, device_id_type=pl.DeviceIdType.MESH)
        if when is None:
            signal()
            total = total + 1
        else:
            pl.when(when)(signal)
            total = total + when.astype(jnp.int32)
    pl.semaphore_wait(barrier, total)


def gather_partners(me):
    pairs = [(me.at(c=1 - me.c), None)]
    for by in (1, -1):
        pairs += [(me.at(y=ring(me.y, by)), None), (me.at(x=ring(me.x, by)), None),
                  (me.at(h=ring(me.h, by)), None)]
    pairs += [(me.at(z=me.z + 1), me.z < 3), (me.at(z=me.z - 1), me.z > 0)]
    return pairs


def gather_steps(me, sends, full, slab, pole_sems, twin_sems, slab_sems, weigh):
    rows, depth = full[0].shape[0] // 32, slab.shape[1] // 16
    twin = me.at(c=1 - me.c)
    pending = []

    def pole_view(half, y, z, c):
        at = ((y * 4 + z) * 2 + c) * rows
        return full[half].at[pl.ds(pl.multiple_of(at, rows), rows)]

    def send_pole(half, y, z, device, when=None):
        sends.start(lambda: pole_view(half, y, z, me.c), lambda: pole_view(half, y, z, me.c),
                    lambda: pole_sems.at[(y * 4 + z) * 2 + half], device, when)

    def send_twin(half, y, z, when=None):
        sends.start(lambda: pole_view(half, y, z, me.c), lambda: pole_view(half, y, z, me.c),
                    lambda: twin_sems.at[(y * 4 + z) * 2 + half], twin, when)

    def await_pole(half, y, z, when=None):
        def waits():
            arrived(pole_view(half, y, z, me.c), pole_sems.at[(y * 4 + z) * 2 + half], twin)
        waits() if when is None else pl.when(when)(waits)

    def slab_view(half, x, h):
        return slab.at[half, pl.ds(pl.multiple_of((x * 4 + h) * depth, depth), depth)]

    def send_slab(half, x, h, device):
        sends.start(lambda: slab_view(half, x, h), lambda: slab_view(half, x, h),
                    lambda: slab_sems.at[(x * 4 + h) * 2 + half], device)

    def await_slab(half, x, h):
        arrived(slab_view(half, x, h), slab_sems.at[(x * 4 + h) * 2 + half], twin)

    up, down = me.at(y=ring(me.y, 1)), me.at(y=ring(me.y, -1))
    east, west = me.at(x=ring(me.x, 1)), me.at(x=ring(me.x, -1))
    far, near = me.at(h=ring(me.h, 1)), me.at(h=ring(me.h, -1))
    right, left = me.at(z=me.z + 1), me.at(z=me.z - 1)

    def drain(count=None):
        for y, z, when in pending[:count]:
            def waits_and_weighs(y=y, z=z):
                for half in (0, 1):
                    arrived(pole_view(half, y, z, 1 - me.c), twin_sems.at[(y * 4 + z) * 2 + half], twin)
                weigh(y, z)
            waits_and_weighs() if when is None else pl.when(when)(waits_and_weighs)
        del pending[:count]

    def along_y(z, when=None):
        for half in (0, 1):
            send_pole(half, me.y, z, up, when)
            send_pole(half, me.y, z, down, when)

    def to_twin(y, z, when=None):
        for half in (0, 1):
            send_twin(half, y, z, when)
        pending.append((y, z, when))

    def from_y(z, when=None):
        below, above = ring(me.y, -1), ring(me.y, 1)
        await_pole(0, below, z, when)
        send_pole(0, below, z, up, when)
        await_pole(1, above, z, when)
        send_pole(1, above, z, down, when)
        await_pole(1, below, z, when)
        await_pole(0, above, z, when)
        to_twin(below, z, when)
        to_twin(above, z, when)

    def from_opposite(z, when=None):
        across = ring(me.y, 2)
        for half in (0, 1):
            await_pole(half, across, z, when)
        to_twin(across, z, when)

    def from_z(by):
        for sign, onward, can in ((-1, right, me.z < 3), (1, left, me.z > 0)):
            z = me.z + sign * by
            there = (z >= 0) & (z <= 3)
            for half in (0, 1):
                await_pole(half, me.y, z, there)
                if by < 3:
                    send_pole(half, me.y, z, onward, there & can)
            along_y(z, there)
            to_twin(me.y, z, there)

    def sources(by):
        return [(z, (z >= 0) & (z <= 3)) for z in (me.z - by, me.z + by)]

    def along_x(h):
        for half in (0, 1):
            send_slab(half, me.x, h, east)
            send_slab(half, me.x, h, west)

    def from_x(h):
        behind, ahead = ring(me.x, -1), ring(me.x, 1)
        await_slab(0, behind, h)
        send_slab(0, behind, h, east)
        await_slab(1, ahead, h)
        send_slab(1, ahead, h, west)
        await_slab(1, behind, h)
        await_slab(0, ahead, h)

    def from_x_opposite(h):
        for half in (0, 1):
            await_slab(half, ring(me.x, 2), h)

    behind, ahead, across = ring(me.h, -1), ring(me.h, 1), ring(me.h, 2)

    def first():
        for half in (0, 1):
            send_pole(half, me.y, me.z, right, me.z < 3)
            send_pole(half, me.y, me.z, left, me.z > 0)
        along_y(me.z)
        to_twin(me.y, me.z)

    def slab_first():
        for half in (0, 1):
            send_slab(half, me.x, me.h, far)
            send_slab(half, me.x, me.h, near)
        along_x(me.h)

    def slab_second():
        await_slab(0, me.x, behind)
        send_slab(0, me.x, behind, far)
        await_slab(1, me.x, ahead)
        send_slab(1, me.x, ahead, near)
        await_slab(1, me.x, behind)
        await_slab(0, me.x, ahead)
        along_x(behind)
        along_x(ahead)

    def slab_third():
        for half in (0, 1):
            await_slab(half, me.x, across)
        along_x(across)

    def rest():
        from_z(1)
        slab_first()
        drain(1)
        from_z(2)
        from_y(me.z)
        drain(2)
        from_z(3)
        for z, there in sources(1):
            from_y(z, there)
        from_opposite(me.z)
        slab_second()
        drain(4)
        for z, there in sources(2):
            from_y(z, there)
        from_x(me.h)
        drain(4)
        for z, there in sources(1):
            from_opposite(z, there)
        slab_third()
        from_x(behind)
        from_x(ahead)
        drain(5)
        for z, there in sources(3):
            from_y(z, there)
        for z, there in sources(2):
            from_opposite(z, there)
        from_x(across)
        drain(len(pending) - 3)
        for h in (me.h, behind, ahead, across):
            from_x_opposite(h)

    def last():
        for z, there in sources(3):
            from_opposite(z, there)
        drain()

    return first, rest, last


def far_partners(me):
    pairs = [(me.at(x=ring(me.x, 2)), None), (me.at(h=ring(me.h, 2)), None), (me.at(y=ring(me.y, 2)), None)]
    for by in (1, 2, 3):
        pairs += [(me.at(y=ring(me.y, by), c=1 - me.c), None)]
        z = ring(me.z, by)
        pairs += [(me.at(z=z), jnp.abs(z - me.z) > 1)]
    return pairs


def reduce_steps(me, sends, part, out, out_twin, mine, twin, x_in, x_sum, y_in, y_sum, h_in, z_all, last, sems):
    other = me.at(c=1 - me.c)

    def await_(view, slot):
        arrived(view, sems.at[slot], other)

    def send(src, dst, slot, device):
        sends.start(lambda: src, lambda: dst, lambda: sems.at[slot], device)

    width = mine.shape[-1]
    theirs = pl.ds(pl.multiple_of((1 - me.c) * width, width), width)
    ours = pl.ds(pl.multiple_of(me.c * width, width), width)
    for by in (2, 1, 3, 0):
        x = ring(me.x, by)
        block = pl.ds(pl.multiple_of(x * 128, 128), 128)
        out_twin[x] = part[block, theirs].astype(jnp.bfloat16)
        send(out_twin.at[x], twin.at[x], by, other)
    for by in (2, 1, 3, 0):
        x = ring(me.x, by)
        block = pl.ds(pl.multiple_of(x * 128, 128), 128)
        await_(twin.at[x], by)
        summed = part[block, ours] + twin[x].astype(jnp.float32)
        if by:
            mine[x] = summed.astype(jnp.bfloat16)
            send(mine.at[x], x_in.at[by - 1], 4 + by - 1, me.at(x=x))
        else:
            x_sum[...] = summed.reshape(x_sum.shape)
    total = x_sum[...]
    for by in (3, 1, 2):
        await_(x_in.at[by - 1], 4 + by - 1)
        total = total + x_in[by - 1].astype(jnp.float32).reshape(x_sum.shape)
    x_sum[...] = total
    for by in (2, 1, 3):
        y = ring(me.y, by)
        send(x_sum.at[:, y], y_in.at[by - 1], 7 + by - 1, me.at(y=y))
    total = x_sum[:, me.y]
    for by in (3, 1, 2):
        await_(y_in.at[by - 1], 7 + by - 1)
        total = total + y_in[by - 1]
    y_sum[...] = total
    for by in (2, 1, 3):
        h = ring(me.h, by)
        send(y_sum.at[h], h_in.at[by - 1], 10 + by - 1, me.at(h=h))
    total = y_sum[me.h]
    for by in (3, 1, 2):
        await_(h_in.at[by - 1], 10 + by - 1)
        total = total + h_in[by - 1]
    z_all[me.z] = total
    for by in (2, 1, 3):
        z = ring(me.z, by)
        send(z_all.at[me.z], z_all.at[me.z], 13 + me.z, me.at(z=z))
    for by in (3, 1, 2):
        z = ring(me.z, by)
        await_(z_all.at[z], 13 + z)
    last[...] = (z_all[0] + z_all[1]) + (z_all[2] + z_all[3])
    rows = pl.ds(pl.multiple_of(me.y * 8, 8), 8)
    slot = 17 + me.y * 2 + me.c
    for by in (2, 1, 3):
        y = ring(me.y, by)
        send(last, out.at[rows, ours], slot, me.at(y=y))
        send(last, out.at[rows, ours], slot, me.at(y=y, c=1 - me.c))
    send(last, out.at[rows, ours], slot, other)
    out[rows, ours] = last[...]
    for by in (0, 1, 2, 3):
        y = ring(me.y, by)
        there = pl.ds(pl.multiple_of(y * 8, 8), 8)
        if by:
            await_(out.at[there, ours], 17 + y * 2 + me.c)
        await_(out.at[there, theirs], 17 + y * 2 + 1 - me.c)


def reduce_scratch():
    f32, bf16 = jnp.float32, jnp.bfloat16
    return [
        pltpu.VMEM((4, 128, 256), bf16), pltpu.VMEM((4, 128, 256), bf16),
        pltpu.VMEM((4, 128, 256), bf16), pltpu.VMEM((3, 128, 256), bf16),
        pltpu.VMEM((4, 4, 8, 256), f32),
        pltpu.VMEM((3, 4, 8, 256), f32), pltpu.VMEM((4, 8, 256), f32),
        pltpu.VMEM((3, 8, 256), f32), pltpu.VMEM((4, 8, 256), f32),
        pltpu.VMEM((8, 256), f32), pltpu.SemaphoreType.DMA((25,)),
    ]


def chosen_band(order, mags, slot, occupied):
    lanes = lax.broadcasted_iota(jnp.int32, order.shape, 1)
    band = jnp.sum(jnp.where(lanes == slot, order, 0), axis=1, keepdims=True)
    magnitude = jnp.sum(jnp.where(lanes == band, mags, 0.0), axis=1, keepdims=True)
    return magnitude, jnp.where(band < occupied, 1.0, -1.0).astype(jnp.float32)


def whole_kernel(normalizer, elems_hbm, res_hbm, pole_hbm, index, order, mags, out,
                 elems, split, poles, ress, slab, slab_n, weights, part,
                 send_sems, pole_sems, twin_sems, slab_sems, own_sems, *reduce_refs):
    me = Place()
    rows, width = pole_hbm.shape
    states = elems.shape[0]
    depth = index.shape[1]
    pool, col = lax.axis_index("pool"), lax.axis_index("col")
    bf16, f32 = jnp.bfloat16, jnp.float32
    at = pl.ds(pl.multiple_of(pool * rows, rows), rows)
    loads = [
        pltpu.make_async_copy(pole_hbm, poles.at[at], own_sems.at[0]),
        pltpu.make_async_copy(res_hbm, ress.at[at], own_sems.at[1]),
        pltpu.make_async_copy(elems_hbm, elems, own_sems.at[2]),
    ]
    for load in loads:
        load.start()
    greet(gather_partners(me) + far_partners(me))
    sends = Sends(send_sems)
    bands = [chosen_band(order[...], mags[...], pool * 2 + j, order.shape[1] // 4) for j in (0, 1)]

    def weigh(y, z):
        first_row = pl.multiple_of((y * 4 + z) * 2 * rows, 2 * rows)

        def chunk(k, carry):
            here = pl.ds(first_row, 2 * rows), pl.ds(pl.multiple_of(k * 256, 256), 256)
            pole, res = poles[here].astype(f32), ress[here].astype(f32)
            for j, (magnitude, parity) in enumerate(bands):
                gap = parity * (pole + magnitude)
                scaled = res * gap / (gap * gap + broadening * broadening)
                weights[(j,) + here] = scaled.astype(bf16)
            return carry

        lax.fori_loop(0, width // 256, chunk, 0)

    first, rest, last = gather_steps(
        me, sends, (poles, ress), slab, pole_sems, twin_sems, slab_sems, weigh)
    loads[0].wait()
    loads[1].wait()
    first()

    loads[2].wait()
    to = lax.broadcasted_iota(jnp.int32, (256, 256), 0)
    came = lax.broadcasted_iota(jnp.int32, (256, 256), 1)
    swap = (came == (to % 128) * 2 + to // 128).astype(bf16)

    def part_by_slot(i, carry):
        n = pl.ds(pl.multiple_of(i * 128, 128), 128)
        pairs = elems[n].reshape(256, width)
        sorted_rows = jnp.dot(swap, pairs, preferred_element_type=f32).astype(bf16)
        split[0, n] = sorted_rows[:128]
        split[1, n] = sorted_rows[128:]
        return carry

    lax.fori_loop(0, states // 128, part_by_slot, 0)
    diagonal = lax.broadcasted_iota(jnp.int32, (depth, depth), 0) == lax.broadcasted_iota(
        jnp.int32, (depth, depth), 1)
    local = jnp.sum(jnp.where(diagonal, index[...] - col * width, 0), axis=1, keepdims=True)
    chosen = (lax.broadcasted_iota(jnp.int32, (depth, width), 1) == local).astype(bf16)
    own_slab = pl.ds(pl.multiple_of(col * depth, depth), depth)
    for j in (0, 1):
        slab[j, own_slab] = lax.dot_general(
            chosen, split[j], (((1,), (1,)), ((), ())), preferred_element_type=f32).astype(bf16)

    rest()
    for j in (0, 1):
        slab_n[j] = slab[j].T
    last()

    half = states // 2
    for top in (0, half):
        def chunk(k, carry):
            here = pl.ds(pl.multiple_of(k * 256, 256), 256)
            total = None
            for j in (0, 1):
                mixed = jnp.dot(slab_n[j, top:top + half], weights[j, :, here],
                                preferred_element_type=f32).astype(bf16)
                term = lax.dot_general(mixed, split[j, :, here], (((1,), (1,)), ((), ())),
                                       preferred_element_type=f32)
                total = term if total is None else total + term
            part[top:top + half] += total
            return carry

        part[top:top + half] = jnp.zeros((half, states), f32)
        lax.fori_loop(0, width // 256, chunk, 0)
    part[...] = part[...] * normalizer
    reduce_steps(me, sends, part, out, *reduce_refs)
    sends.finish()


def on_device(matrix_elems, residue, pole_freq, slab_index, band_order, band_mag):
    states, members, width = matrix_elems.shape
    rows, slab_rows = residue.shape[0], residue.shape[0] * 32
    bands = band_order.shape[0]
    normalizer = float(1.0 / np.sqrt(np.float32(bands * slab_rows * width * 16)))
    dma, vmem, anywhere = pltpu.SemaphoreType.DMA, pltpu.VMEM, pl.BlockSpec(memory_space=pl.ANY)
    whole = pl.BlockSpec(memory_space=pltpu.VMEM)
    bf16 = jnp.bfloat16
    return pl.pallas_call(
        functools.partial(whole_kernel, normalizer),
        out_shape=jax.ShapeDtypeStruct((states // 16, states), jnp.float32),
        in_specs=[anywhere] * 3 + [whole] * 3,
        out_specs=whole,
        scratch_shapes=[
            vmem((states, members, width), bf16), vmem((members, states, width), bf16),
            vmem((slab_rows, width), bf16), vmem((slab_rows, width), bf16),
            vmem((members, slab_rows, states), bf16), vmem((members, states, slab_rows), bf16),
            vmem((members, slab_rows, width), bf16), vmem((states, states), jnp.float32),
            dma((SENDS,)), dma((32,)), dma((32,)), dma((32,)), dma((3,)),
        ] + reduce_scratch(),
        compiler_params=pltpu.CompilerParams(
            collective_id=0, has_side_effects=True, vmem_limit_bytes=60 * 2**20),
    )(matrix_elems, residue, pole_freq, slab_index[None], band_order[None], band_mag[None])


def solution(mesh):
    placed = (P(None, "pool", "col"), P("pool", "col"), P("pool", "col"), P("col"), P(), P())
    return jax.shard_map(
        on_device, mesh=mesh, in_specs=placed, out_specs=P("col", None), check_vma=False
    )
```

time: 142 us -> 107 us (0.75)
  matrix products: 19.5 us -> 0 us
  other arithmetic: 13.1 us -> 0 us
  local copies, waits for them, and re-layouts: 3.29 us -> 1.47 us
    dot_general x2 -> x0, matrix products: 19.5 us -> none  [the longest x1 14.8 us: on_device(): jnp.einsum('jng,mjg->nm', mixed_rows, matrix_elems, preferred_element_typ...]
    convert_element_type x2 -> x0, other arithmetic: 10.9 us -> none  [the longest x1 6.64 us: pole_weights(): res_rows.astype(jnp.float32)[None] * signed_gap]
    unnamed x7 -> x1, local copies, waits for them, and re-layouts: 3.29 us -> 1.47 us
    pallas_call x2 -> x1, Pallas kernels: 106 us -> 106 us  [on_device(): pl.pallas_call(functools.partial(whole_kernel, normalizer), out_shape=jax...]
where the time goes in v2:
time: 107 us
  Pallas kernels  106 us (99%)
  local copies, waits for them, and re-layouts  1.47 us (1%)
    pallas_call x1, Pallas kernels, on_device(): pl.pallas_call(functools.partial(whole_kernel, normalizer), out_shape=jax...  106 us

profile of v2, /device:TPU:1, one launch (start us, length us, event | category | flops | bytes accessed | tf_op | source)
XLA Modules:
  0.0 107.3 jit_solution(5830197987741929446)
XLA Ops:
  0.0 105.8 %shard_map.64 = f32[32,512]{1,0:T(8,128)} custom-call(bf16[512,2,2048]{2,1,0:T(2,128)(2,1)} %elems_hbm.1, bf16[32,2048]{1,0:T(8,128)(2,1)} %res_hbm.1, bf16[32,2048]{1,0:T(8,128)(2,1)} %pole_hbm.1, s32[1,64]{1,0:T(1,128)} %bitcast.3, s32[1,64]{1,0:T(1,128)} %bitcast.4, f32[1,64]{1,0:T(1,128)} %bitcast.5), custom_call_target="tpu_custom_call" | custom-call | tf_op jit(solution)/shard_map/pallas_call | solution.py:461
  105.8 1.5 %copy.8 = f32[32,512]{1,0:T(8,128)} copy(f32[32,512]{1,0:T(8,128)} %shard_map.64) | data formatting | bytes 131072

commit v3 on v2

--- a/solution.py
+++ b/solution.py
@@ -89,7 +89,6 @@
 def gather_steps(me, sends, full, slab, pole_sems, twin_sems, slab_sems, weigh):
     rows, depth = full[0].shape[0] // 32, slab.shape[1] // 16
     twin = me.at(c=1 - me.c)
-    pending = []
 
     def pole_view(half, y, z, c):
         at = ((y * 4 + z) * 2 + c) * rows
@@ -123,14 +122,18 @@
     far, near = me.at(h=ring(me.h, 1)), me.at(h=ring(me.h, -1))
     right, left = me.at(z=me.z + 1), me.at(z=me.z - 1)
 
-    def drain(count=None):
-        for y, z, when in pending[:count]:
-            def waits_and_weighs(y=y, z=z):
+    def digest(y, by):
+        def block(i, carry):
+            z = me.z + (2 * i - 1) * by
+
+            @pl.when((z >= 0) & (z <= 3))
+            def _():
                 for half in (0, 1):
                     arrived(pole_view(half, y, z, 1 - me.c), twin_sems.at[(y * 4 + z) * 2 + half], twin)
                 weigh(y, z)
-            waits_and_weighs() if when is None else pl.when(when)(waits_and_weighs)
-        del pending[:count]
+            return carry
+
+        lax.fori_loop(0, 2 if by else 1, block, 0)
 
     def along_y(z, when=None):
         for half in (0, 1):
@@ -140,7 +143,6 @@
     def to_twin(y, z, when=None):
         for half in (0, 1):
             send_twin(half, y, z, when)
-        pending.append((y, z, when))
 
     def from_y(z, when=None):
         below, above = ring(me.y, -1), ring(me.y, 1)
@@ -204,7 +206,6 @@
         for half in (0, 1):
             send_slab(half, me.x, me.h, far)
             send_slab(half, me.x, me.h, near)
-        along_x(me.h)
 
     def slab_second():
         await_slab(0, me.x, behind)
@@ -221,42 +222,56 @@
             await_slab(half, me.x, across)
         along_x(across)
 
+    below, above, opposite = ring(me.y, -1), ring(me.y, 1), ring(me.y, 2)
+
+    def all_from_y(by):
+        for z, there in sources(by):
+            from_y(z, there)
+
+    def all_from_opposite(by):
+        for z, there in sources(by):
+            from_opposite(z, there)
+
     def rest():
         from_z(1)
+        along_x(me.h)
+        digest(me.y, 0)
+        from_z(2)
         slab_first()
-        drain(1)
-        from_z(2)
         from_y(me.z)
-        drain(2)
+        digest(me.y, 1)
         from_z(3)
-        for z, there in sources(1):
-            from_y(z, there)
         from_opposite(me.z)
+        all_from_y(1)
+        digest(below, 0)
+        digest(above, 0)
+        digest(opposite, 0)
+        all_from_opposite(1)
+        all_from_y(2)
+        digest(me.y, 2)
+        digest(below, 1)
         slab_second()
-        drain(4)
-        for z, there in sources(2):
-            from_y(z, there)
+        digest(above, 1)
         from_x(me.h)
-        drain(4)
-        for z, there in sources(1):
-            from_opposite(z, there)
+        all_from_opposite(2)
+        all_from_y(3)
+        digest(me.y, 3)
+        digest(opposite, 1)
         slab_third()
         from_x(behind)
         from_x(ahead)
-        drain(5)
-        for z, there in sources(3):
-            from_y(z, there)
-        for z, there in sources(2):
-            from_opposite(z, there)
+        digest(below, 2)
         from_x(across)
-        drain(len(pending) - 3)
+        digest(above, 2)
         for h in (me.h, behind, ahead, across):
             from_x_opposite(h)
 
     def last():
-        for z, there in sources(3):
-            from_opposite(z, there)
-        drain()
+        digest(opposite, 2)
+        digest(below, 3)
+        all_from_opposite(3)
+        digest(above, 3)
+        digest(opposite, 3)
 
     return first, rest, last
 
@@ -270,7 +285,7 @@
     return pairs
 
 
-def reduce_steps(me, sends, part, out, out_twin, mine, twin, x_in, x_sum, y_in, y_sum, h_in, z_all, last, sems):
+def reduce_steps(me, sends, product, part, out, out_twin, mine, twin, x_in, x_sum, y_in, y_sum, h_in, z_all, last, sems):
     other = me.at(c=1 - me.c)
 
     def await_(view, slot):
@@ -285,6 +300,7 @@
     for by in (2, 1, 3, 0):
         x = ring(me.x, by)
         block = pl.ds(pl.multiple_of(x * 128, 128), 128)
+        product(block)
         out_twin[x] = part[block, theirs].astype(jnp.bfloat16)
         send(out_twin.at[x], twin.at[x], by, other)
     for by in (2, 1, 3, 0):
@@ -361,7 +377,7 @@
 
 
 def whole_kernel(normalizer, elems_hbm, res_hbm, pole_hbm, index, order, mags, out,
-                 elems, split, poles, ress, slab, slab_n, weights, part,
+                 elems, split, poles, ress, slab, slab_n, weights, mixed, part,
                  send_sems, pole_sems, twin_sems, slab_sems, own_sems, *reduce_refs):
     me = Place()
     rows, width = pole_hbm.shape
@@ -385,15 +401,19 @@
         first_row = pl.multiple_of((y * 4 + z) * 2 * rows, 2 * rows)
 
         def chunk(k, carry):
-            here = pl.ds(first_row, 2 * rows), pl.ds(pl.multiple_of(k * 256, 256), 256)
-            pole, res = poles[here].astype(f32), ress[here].astype(f32)
+            block = pl.ds(first_row, 2 * rows)
+            lanes = pl.ds(pl.multiple_of(k * 256, 256), 256)
+            pole, res = poles[block, lanes].astype(f32), ress[block, lanes].astype(f32)
             for j, (magnitude, parity) in enumerate(bands):
                 gap = parity * (pole + magnitude)
                 scaled = res * gap / (gap * gap + broadening * broadening)
-                weights[(j,) + here] = scaled.astype(bf16)
+                weights[j, :, lanes] = scaled.astype(bf16)
             return carry
 
         lax.fori_loop(0, width // 256, chunk, 0)
+        for j in (0, 1):
+            mixed[j, pl.ds(first_row, 2 * rows)] = lax.dot_general(
+                weights[j], split[j], (((1,), (1,)), ((), ())), preferred_element_type=f32).astype(bf16)
 
     first, rest, last = gather_steps(
         me, sends, (poles, ress), slab, pole_sems, twin_sems, slab_sems, weigh)
@@ -429,24 +449,12 @@
         slab_n[j] = slab[j].T
     last()
 
-    half = states // 2
-    for top in (0, half):
-        def chunk(k, carry):
-            here = pl.ds(pl.multiple_of(k * 256, 256), 256)
-            total = None
-            for j in (0, 1):
-                mixed = jnp.dot(slab_n[j, top:top + half], weights[j, :, here],
-                                preferred_element_type=f32).astype(bf16)
-                term = lax.dot_general(mixed, split[j, :, here], (((1,), (1,)), ((), ())),
-                                       preferred_element_type=f32)
-                total = term if total is None else total + term
-            part[top:top + half] += total
-            return carry
-
-        part[top:top + half] = jnp.zeros((half, states), f32)
-        lax.fori_loop(0, width // 256, chunk, 0)
-    part[...] = part[...] * normalizer
-    reduce_steps(me, sends, part, out, *reduce_refs)
+    def product(block):
+        for j in (0, 1):
+            term = jnp.dot(slab_n[j, block], mixed[j], preferred_element_type=f32) * normalizer
+            part[block] = term if j == 0 else part[block] + term
+
+    reduce_steps(me, sends, product, part, out, *reduce_refs)
     sends.finish()
 
 
@@ -467,7 +475,8 @@
             vmem((states, members, width), bf16), vmem((members, states, width), bf16),
             vmem((slab_rows, width), bf16), vmem((slab_rows, width), bf16),
             vmem((members, slab_rows, states), bf16), vmem((members, states, slab_rows), bf16),
-            vmem((members, slab_rows, width), bf16), vmem((states, states), jnp.float32),
+            vmem((members, 2 * rows, width), bf16), vmem((members, slab_rows, states), bf16),
+            vmem((states, states), jnp.float32),
             dma((SENDS,)), dma((32,)), dma((32,)), dma((32,)), dma((3,)),
         ] + reduce_scratch(),
         compiler_params=pltpu.CompilerParams(

time: 107 us -> 111 us (1.037); the launches traced: 107 us -> 110 us
  Pallas kernels: 106 us -> 108 us
    pallas_call x1, Pallas kernels: 106 us -> 108 us  [on_device(): pl.pallas_call(functools.partial(whole_kernel, normalizer), out_shape=jax...]
where the time goes in v3:
time: 111 us; the launch traced here: 110 us
  Pallas kernels  108 us (97%)
  local copies, waits for them, and re-layouts  1.47 us (1%)
    pallas_call x1, Pallas kernels, on_device(): pl.pallas_call(functools.partial(whole_kernel, normalizer), out_shape=jax...  108 us

profile of v3, /device:TPU:1, one launch (start us, length us, event | category | flops | bytes accessed | tf_op | source)
XLA Modules:
  0.0 109.7 jit_solution(1850265184714465757)
XLA Ops:
  0.0 108.2 %shard_map.64 = f32[32,512]{1,0:T(8,128)} custom-call(bf16[512,2,2048]{2,1,0:T(2,128)(2,1)} %elems_hbm.1, bf16[32,2048]{1,0:T(8,128)(2,1)} %res_hbm.1, bf16[32,2048]{1,0:T(8,128)(2,1)} %pole_hbm.1, s32[1,64]{1,0:T(1,128)} %bitcast.3, s32[1,64]{1,0:T(1,128)} %bitcast.4, f32[1,64]{1,0:T(1,128)} %bitcast.5), custom_call_target="tpu_custom_call" | custom-call | tf_op jit(solution)/shard_map/pallas_call | solution.py:469
  108.2 1.5 %copy.8 = f32[32,512]{1,0:T(8,128)} copy(f32[32,512]{1,0:T(8,128)} %shard_map.64) | data formatting | bytes 131072

commit v4 on v3

--- a/solution.py
+++ b/solution.py
@@ -86,7 +86,7 @@
     return pairs
 
 
-def gather_steps(me, sends, full, slab, pole_sems, twin_sems, slab_sems, weigh):
+def gather_steps(me, sends, full, slab, pole_sems, twin_sems, slab_sems, weigh, row_products):
     rows, depth = full[0].shape[0] // 32, slab.shape[1] // 16
     twin = me.at(c=1 - me.c)
 
@@ -206,6 +206,7 @@
         for half in (0, 1):
             send_slab(half, me.x, me.h, far)
             send_slab(half, me.x, me.h, near)
+        along_x(me.h)
 
     def slab_second():
         await_slab(0, me.x, behind)
@@ -234,44 +235,47 @@
 
     def rest():
         from_z(1)
-        along_x(me.h)
+        slab_first()
         digest(me.y, 0)
         from_z(2)
-        slab_first()
         from_y(me.z)
         digest(me.y, 1)
         from_z(3)
+        all_from_y(1)
         from_opposite(me.z)
-        all_from_y(1)
+        slab_second()
         digest(below, 0)
         digest(above, 0)
+        all_from_y(2)
+        from_x(me.h)
         digest(opposite, 0)
+        digest(me.y, 2)
         all_from_opposite(1)
-        all_from_y(2)
-        digest(me.y, 2)
-        digest(below, 1)
-        slab_second()
-        digest(above, 1)
-        from_x(me.h)
-        all_from_opposite(2)
-        all_from_y(3)
-        digest(me.y, 3)
-        digest(opposite, 1)
         slab_third()
         from_x(behind)
         from_x(ahead)
+        digest(below, 1)
+        digest(above, 1)
+        digest(me.y, 3)
+        all_from_y(3)
+        all_from_opposite(2)
+        from_x(across)
+        digest(opposite, 1)
         digest(below, 2)
-        from_x(across)
         digest(above, 2)
+        row_products(me.y)
         for h in (me.h, behind, ahead, across):
             from_x_opposite(h)
 
     def last():
+        digest(below, 3)
+        digest(above, 3)
+        row_products(below)
+        all_from_opposite(3)
+        row_products(above)
         digest(opposite, 2)
-        digest(below, 3)
-        all_from_opposite(3)
-        digest(above, 3)
         digest(opposite, 3)
+        row_products(opposite)
 
     return first, rest, last
 
@@ -407,16 +411,19 @@
             for j, (magnitude, parity) in enumerate(bands):
                 gap = parity * (pole + magnitude)
                 scaled = res * gap / (gap * gap + broadening * broadening)
-                weights[j, :, lanes] = scaled.astype(bf16)
+                weights[j, block, lanes] = scaled.astype(bf16)
             return carry
 
         lax.fori_loop(0, width // 256, chunk, 0)
+
+    def row_products(y):
+        block = pl.ds(pl.multiple_of(y * 8 * rows, 8 * rows), 8 * rows)
         for j in (0, 1):
-            mixed[j, pl.ds(first_row, 2 * rows)] = lax.dot_general(
-                weights[j], split[j], (((1,), (1,)), ((), ())), preferred_element_type=f32).astype(bf16)
+            mixed[j, block] = lax.dot_general(
+                weights[j, block], split[j], (((1,), (1,)), ((), ())), preferred_element_type=f32).astype(bf16)
 
     first, rest, last = gather_steps(
-        me, sends, (poles, ress), slab, pole_sems, twin_sems, slab_sems, weigh)
+        me, sends, (poles, ress), slab, pole_sems, twin_sems, slab_sems, weigh, row_products)
     loads[0].wait()
     loads[1].wait()
     first()
@@ -475,7 +482,7 @@
             vmem((states, members, width), bf16), vmem((members, states, width), bf16),
             vmem((slab_rows, width), bf16), vmem((slab_rows, width), bf16),
             vmem((members, slab_rows, states), bf16), vmem((members, states, slab_rows), bf16),
-            vmem((members, 2 * rows, width), bf16), vmem((members, slab_rows, states), bf16),
+            vmem((members, slab_rows, width), bf16), vmem((members, slab_rows, states), bf16),
             vmem((states, states), jnp.float32),
             dma((SENDS,)), dma((32,)), dma((32,)), dma((32,)), dma((3,)),
         ] + reduce_scratch(),

time: 111 us -> 101 us (0.910); the launches traced: 110 us -> 101 us
  Pallas kernels: 108 us -> 99.8 us
    pallas_call x1, Pallas kernels: 108 us -> 99.8 us  [on_device(): pl.pallas_call(functools.partial(whole_kernel, normalizer), out_shape=jax...]
where the time goes in v4:
time: 101 us
  Pallas kernels  99.8 us (99%)
  local copies, waits for them, and re-layouts  1.47 us (1%)
    pallas_call x1, Pallas kernels, on_device(): pl.pallas_call(functools.partial(whole_kernel, normalizer), out_shape=jax...  99.8 us

profile of v4, /device:TPU:1, one launch (start us, length us, event | category | flops | bytes accessed | tf_op | source)
XLA Modules:
  0.0 101.3 jit_solution(12495943959596121472)
XLA Ops:
  0.0 99.8 %shard_map.64 = f32[32,512]{1,0:T(8,128)} custom-call(bf16[512,2,2048]{2,1,0:T(2,128)(2,1)} %elems_hbm.1, bf16[32,2048]{1,0:T(8,128)(2,1)} %res_hbm.1, bf16[32,2048]{1,0:T(8,128)(2,1)} %pole_hbm.1, s32[1,64]{1,0:T(1,128)} %bitcast.3, s32[1,64]{1,0:T(1,128)} %bitcast.4, f32[1,64]{1,0:T(1,128)} %bitcast.5), custom_call_target="tpu_custom_call" | custom-call | tf_op jit(solution)/shard_map/pallas_call | solution.py:476
  99.8 1.5 %copy.8 = f32[32,512]{1,0:T(8,128)} copy(f32[32,512]{1,0:T(8,128)} %shard_map.64) | data formatting | bytes 131072
